TPU v7x, 512 devices: a whole 4x4x16 slice. The times are simulated.
512 devices in a mesh: dp: 32 (over z, core), seq: 16 (over y, x).
Axes of the slice: x: 4, y: 4, z: 16, core: 2. Of those that a mesh axis runs over, the one named last changes fastest.
Arguments:
- tokens: bfloat16 [65536, 1280], P(('dp', 'seq')), parts along dimension 0, may hold values from -6 to 6
- segment_ids: int32 [65536], P('dp'), parts along dimension 0, may hold values from 0 to 31, as said below
- w_qkv: bfloat16 [1280, 3840], P(None, 'seq')
- w_out: bfloat16 [1280, 1280], P('seq'), may hold values from -0.15625 to 0.15625
- w_merge: bfloat16 [5120, 4096], P(None, 'seq'), may hold values from -0.078125 to 0.078125
- gain_attn: float32 [1280], replicated, may hold values from 0.1 to 1.9
- gain_merge: float32 [1280], replicated, may hold values from 0.1 to 1.9
Outputs:
- merged_out: bfloat16 [16384, 4096], P(('dp', 'seq')), parts along dimension 0
There are 32 independent parts, one for each index of `dp`. A program takes and returns all parts, laid end to end along the dimension named above; an argument that names none is the same for every part. Nothing has to cross between parts.
Inputs may be any that keep to these rules, and one draw needn't show every extreme that they name: `segment_ids`: Non-decreasing along the packed tokens, starting at 0, rising by 0 or 1 from one token to the next, and equal within every aligned group of 4 tokens (an image's 2x2 patch blocks are stored together). There are exactly 32 images.
All inputs are finite; a program needn't handle non-finite values.
Results may differ from a plain program's by a relative error of at most 0.011.
Values may be sent and summed in bfloat16 or wider, within the bound.
No kernel may reach another device: no remote copies, remote signals or barrier semaphores. Data moves between devices by JAX's collectives and lax.ppermute only.
A program may use at most 64 MiB of HBM per device.

v0:
```python
import jax
import jax.numpy as jnp
from jax import lax
from jax.sharding import Mesh
from jax.sharding import PartitionSpec as P

D = 1280
HEADS = 16
HEAD_DIM = 80
SEQ = ("seq_0", "seq_1")
DP_SEQ = ("dp", "seq_0", "seq_1")


def gathered_by_axis(value, axes, dim):
    for axis in reversed(axes):
        value = lax.all_gather(value, axis, axis=dim, tiled=True)
    return value


def layer_norm(vector, scale_gain):
    average = jnp.mean(vector, axis=-1, keepdims=True)
    centred = vector - average
    spread_sq = jnp.mean(centred * centred, axis=-1, keepdims=True)
    return centred * lax.rsqrt(spread_sq + 1e-06) * scale_gain


def per_device(tokens, segment_ids, w_qkv, w_out, w_merge, gain_attn, gain_merge):
    group_size = lax.axis_size(SEQ)
    tok_local = tokens.shape[0]
    all_tokens = tok_local * group_size
    local_heads = HEADS // group_size
    residual = tokens.astype(jnp.float32)
    normed = layer_norm(residual, gain_attn).astype(jnp.bfloat16)
    qkv_rows = jnp.dot(
        lax.all_gather(normed, SEQ, axis=0, tiled=True), w_qkv, preferred_element_type=jnp.float32
    ).astype(jnp.bfloat16)
    qkv = qkv_rows.reshape(all_tokens, local_heads, 3, HEAD_DIM)
    key_rows = qkv[:, :, 1, :]
    value_rows = qkv[:, :, 2, :]
    block_rows = min(512, all_tokens)
    block_count = all_tokens // block_rows
    scale_factor = HEAD_DIM ** (-0.5)

    def masked_scores(queries, query_ids, key_part, key_ids):
        scores = (
            jnp.einsum("qhd,khd->hqk", queries, key_part, preferred_element_type=jnp.float32)
            * scale_factor
        )
        same_image = (query_ids[:, None] == key_ids[None, :])[None, :, :]
        return (jnp.where(same_image, scores, -jnp.inf), same_image)

    def query_block(block_index):
        query_start = block_index * block_rows
        queries = lax.dynamic_slice_in_dim(qkv, query_start, block_rows, 0)[:, :, 0, :]
        query_ids = lax.dynamic_slice_in_dim(segment_ids, query_start, block_rows, 0)
        scores, same_image = masked_scores(queries, query_ids, key_rows, segment_ids)
        row_max = jnp.max(scores, axis=-1, keepdims=True)
        expo = jnp.where(same_image, jnp.exp(scores - row_max), 0.0)
        row_sum = jnp.sum(expo, axis=-1)
        probs = expo.astype(jnp.bfloat16)
        summed = jnp.einsum("hqk,khd->qhd", probs, value_rows, preferred_element_type=jnp.float32)
        result = summed / row_sum.T[:, :, None]
        return result.astype(jnp.bfloat16).reshape(block_rows, local_heads * HEAD_DIM)

    attended = lax.map(query_block, jnp.arange(block_count, dtype=jnp.int32)).reshape(
        all_tokens, local_heads * HEAD_DIM
    )
    back = lax.all_to_all(attended, SEQ, split_axis=0, concat_axis=1, tiled=True)
    projected_attn = jnp.dot(
        back, gathered_by_axis(w_out, SEQ, 0), preferred_element_type=jnp.float32
    )
    hidden = residual + projected_attn
    normed_two = layer_norm(hidden, gain_merge).astype(jnp.bfloat16)
    merged = normed_two.reshape(tok_local // 4, 4 * D)
    column_block = jnp.dot(
        lax.all_gather(merged, SEQ, axis=0, tiled=True), w_merge, preferred_element_type=jnp.float32
    ).astype(jnp.bfloat16)
    return lax.all_to_all(column_block, SEQ, split_axis=0, concat_axis=1, tiled=True)


def solution(mesh):
    torus = Mesh(mesh.devices.reshape(mesh.shape["dp"], 4, 4), ("dp", "seq_0", "seq_1"))
    in_specs = (P(DP_SEQ, None), P("dp"), P(None, SEQ), P(SEQ, None), P(None, SEQ), P(), P())
    out_specs = P(DP_SEQ, None)
    return jax.shard_map(
        per_device, mesh=torus, in_specs=in_specs, out_specs=out_specs, check_vma=False
    )
```

profile of v0, /device:TPU:32, one launch (start us, length us, event | category | flops | bytes accessed | tf_op | source)
XLA Modules:
  0.0 241.4 jit_solution(16823086100214955920)
XLA Ops:
  6.5 1.2 convert_reduce_fusion
  9.0 1.9 fusion.31
  11.0 16.2 %all_gather.13 = bf16[320,1280]{1,0:T(8,128)(2,1)} all-gather(bf16[80,1280]{1,0:T(8,128)(2,1)} %param.12), channel_id=1, replica_groups=mesh['dp'=32,'seq_0'=4,'seq_1'=4] {'seq_1'}, dimensions={0}, use_global_device_ids=true | all-gather | bytes 1024000 | tf_op jit(solution)/shard_map/all_gather | solution.py:16
  27.3 59.5 %all-gather.4.cloned.1.call-done = bf16[2048,1280]{1,0:T(8,128)(2,1)} async-done(((bf16[128,1280]{1,0:T(8,128)(2,1)}), bf16[2048,1280]{1,0:T(8,128)(2,1)}) %all-gather.4.cloned.1.call-update) | async-done | bytes 5242896 | tf_op jit(solution)/shard_map/all_gather | solution.py:35
  86.8 4.2 %convolution_convert_fusion = bf16[2048,240]{0,1:T(8,128)(2,1)S(1)} fusion(bf16[2048,1280]{1,0:T(8,128)(2,1)} %all-gather.4.cloned.1.call-done, bf16[1280,240]{0,1:T(8,128)(2,1)} %param.11), kind=kOutput, calls=%fused_computation.19 | convolution fusion | flops 1258782720 | bytes 6840320 | tf_op jit(solution)/shard_map/dot_general | solution.py:34
  92.0 25.1 %while.10 = (s32[]{:T(128)}, bf16[4,512,80]{1,2,0:T(8,128)(2,1)}, s32[4]{0:T(128)S(1)}, s32[2048]{0:T(1024)S(1)}, bf16[2048,1,3,80]{0,3,2,1:T(8,128)(2,1)}, /*in...) while((s32[]{:T(128)}, bf16[4,512,80]{1,2,0:T(8,128)(2,1)}, ...), condition=%wide.region_5.6_spmd, body=%wide.region_2.5_spmd.sunk | while | flops 352402432 | bytes 13447855 | solution.py:65
  93.3 1.9 fusion.46
  95.2 1.2 fusion.47
  96.4 1.9 fusion.48
  99.5 1.9 fusion.46
  101.4 1.2 fusion.47
  102.7 1.9 fusion.48
  105.8 1.9 fusion.46
  107.7 1.2 fusion.47
  109.0 1.9 fusion.48
  112.1 1.9 fusion.46
  115.3 1.9 fusion.48
  119.2 1.8 copy.16
  121.0 5.3 %all-to-all-start = ((bf16[16,128,80]{1,2,0:T(8,128)(2,1)}), bf16[16,128,80]{1,2,0:T(8,128)(2,1)S(1)}, u32[]{:S(2)}, u32[]{:S(2)}) async-start(bf16[16,128,80]{1,2,0:T(8,128)(2,1)} %copy.16), calls=%async_computation | async-start | bytes 655360 | tf_op jit(solution)/shard_map/all_to_all | solution.py:68
  126.3 14.2 %all-gather.6.cloned.1.call-done = bf16[1280,1280]{1,0:T(8,128)(2,1)} async-done(((bf16[320,1280]{1,0:T(8,128)(2,1)}), bf16[1280,1280]{1,0:T(8,128)(2,1)}) %all-gather.6.cloned.1.call-update) | async-done | bytes 3276816 | tf_op jit(solution)/shard_map/all_gather | solution.py:16
  140.5 2.6 %fusion.32 = (f32[128]{0:T(128)S(1)}, f32[128,1280]{1,0:T(8,128)S(1)}) fusion(bf16[128,1280]{0,1:T(8,128)(2,1)S(1)} %bitcast.64, bf16[1280,1280]{1,0:T(8,128)(2,1)} %all-gather.6.cloned.1.call-done, bf16[128,1280]{1,0:T(8,128)(2,1)S(1)} %copy-done.1), kind=kOutput, calls=%fused_computation.37 | convolution fusion | flops 419921792 | bytes 4588032 | tf_op jit(solution)/shard_map/dot_general | solution.py:69
  144.5 71.9 %all-gather.8.cloned.1.call-done = bf16[512,5120]{1,0:T(8,128)(2,1)} async-done(((bf16[32,5120]{1,0:T(8,128)(2,1)}), bf16[512,5120]{1,0:T(8,128)(2,1)}) %all-gather.8.cloned.1.call-update) | async-done | bytes 5242896 | tf_op jit(solution)/shard_map/all_gather | solution.py:76
  216.4 4.0 %convolution_convert_fusion.1 = bf16[512,256]{1,0:T(8,128)(2,1)S(1)} fusion(bf16[512,5120]{1,0:T(8,128)(2,1)} %all-gather.8.cloned.1.call-done, bf16[5120,256]{1,0:T(8,128)(2,1)S(1)} %copy-done), kind=kOutput, calls=%fused_computation.21 | convolution fusion | flops 1342308352 | bytes 8126464 | tf_op jit(solution)/shard_map/dot_general | solution.py:75
  220.4 13.7 %all_to_all.38 = bf16[16,32,256]{2,1,0:T(8,128)(2,1)S(1)} all-to-all(bf16[16,32,256]{2,1,0:T(8,128)(2,1)S(1)} %bitcast.68), channel_id=1, replica_groups=mesh['dp'=32,'seq_0'=4,'seq_1'=4] {'seq_0','seq_1'}, dimensions={0} | all-to-all | bytes 524288 | tf_op jit(solution)/shard_map/all_to_all | solution.py:78
  (40 shorter events, 10.5 us)
Async XLA Ops:
  6.5 209.9 %copy-start = (bf16[5120,256]{1,0:T(8,128)(2,1)S(1)}, bf16[5120,256]{1,0:T(8,128)(2,1)}, u32[]{:S(2)}) copy-start(bf16[5120,256]{1,0:T(8,128)(2,1)} %param.13) | copy-start | bytes 7864324
  6.5 80.2 %all-gather.4.cloned.1.call-start = ((), (), s32[]{:S(2)}) async-start(), calls=%async_computation.2 | async-start | bytes 5570560 | tf_op jit(solution)/shard_map/all_gather | solution.py:35
  11.0 129.5 %all-gather.6.cloned.1.call-start = ((), (), s32[]{:S(2)}) async-start(), calls=%async_computation.3 | async-start | bytes 4096000 | tf_op jit(solution)/shard_map/all_gather | solution.py:16
  27.3 64.8 %copy-start.3 = (s32[2048]{0:T(1024)S(1)}, s32[2048]{0:T(1024)}, u32[]{:S(2)}) copy-start(s32[2048]{0:T(1024)} %param.10) | copy-start | bytes 24580
  90.9 1.1 copy-start.2
  92.0 48.5 %copy-start.1 = (bf16[128,1280]{1,0:T(8,128)(2,1)S(1)}, bf16[128,1280]{1,0:T(8,128)(2,1)}, u32[]{:S(2)}) copy-start(bf16[128,1280]{1,0:T(8,128)(2,1)} %param.9) | copy-start | bytes 983044
  117.1 26.3 %copy-start.4 = (f32[1280]{0:T(1024)S(1)}, f32[1280]{0:T(1024)}, u32[]{:S(2)}) copy-start(f32[1280]{0:T(1024)} %param.15) | copy-start | bytes 15364
  121.0 19.5 %all-to-all-start = ((bf16[16,128,80]{1,2,0:T(8,128)(2,1)}), bf16[16,128,80]{1,2,0:T(8,128)(2,1)S(1)}, u32[]{:S(2)}, u32[]{:S(2)}) async-start(bf16[16,128,80]{1,2,0:T(8,128)(2,1)} %copy.16), calls=%async_computation | async-start | bytes 655360 | tf_op jit(solution)/shard_map/all_to_all | solution.py:68
  126.2 90.2 %all-gather.8.cloned.1.call-start = ((), (), s32[]{:S(2)}) async-start(), calls=%async_computation.4 | async-start | bytes 5570560 | tf_op jit(solution)/shard_map/all_gather | solution.py:76
Sparse Core Ops, SparseCore 0:
  11.1 75.6 all-gather.3
  88.9 51.5 all-gather.5
  144.6 71.7 all-gather.7
where the time goes:
time: 242 us; the launch traced here: 241 us
  waiting for transfers between devices  146 us (60%)
  blocking collectives  30 us (12%)
  matrix products  25.9 us (11%)
  between operations  13.2 us (5%)
  other arithmetic  9.78 us (4%)
  local copies, waits for them, and re-layouts  9.27 us (4%)
  starting transfers between devices  5.34 us (2%)
    all_gather x1, waiting for transfers between devices, per_device(): lax.all_gather(merged, SEQ, axis=0, tiled=True)  71.9 us
    all_gather x1, waiting for transfers between devices, per_device(): lax.all_gather(normed, SEQ, axis=0, tiled=True)  59.5 us
    all_gather x1, blocking collectives, gathered_by_axis(): value = lax.all_gather(value, axis, axis=dim, tiled=True)  16.2 us
    all_gather x1, waiting for transfers between devices, gathered_by_axis(): value = lax.all_gather(value, axis, axis=dim, tiled=True)  14.2 us
    all_to_all x1, blocking collectives, per_device(): lax.all_to_all(column_block, SEQ, split_axis=0, concat_axis=1, tiled=True)  13.7 us
    dot_general x4, matrix products, masked_scores(): jnp.einsum('qhd,khd->hqk', queries, key_part, preferred_element_type=jnp....  7.64 us
    dot_general x4, matrix products, query_block(): jnp.einsum('hqk,khd->qhd', probs, value_rows, preferred_element_type=jnp....  7.46 us
    all_to_all x1, starting transfers between devices, per_device(): lax.all_to_all(attended, SEQ, split_axis=0, concat_axis=1, tiled=True)  5.25 us
  transfers between devices with their start and end apart: 4, of which 3 were waited for; matrix products, arithmetic and copies ran while one was open for 13% of the time, Pallas kernels for 0%

commit v1 on v0

--- a/solution.py
+++ b/solution.py
@@ -32,7 +32,11 @@
     residual = tokens.astype(jnp.float32)
     normed = layer_norm(residual, gain_attn).astype(jnp.bfloat16)
     qkv_rows = jnp.dot(
-        lax.all_gather(normed, SEQ, axis=0, tiled=True), w_qkv, preferred_element_type=jnp.float32
+        jnp.concatenate(
+            lax.all_to_all(jnp.stack([normed] * lax.axis_size(SEQ)), SEQ, 0, 0), axis=0
+        ),
+        w_qkv,
+        preferred_element_type=jnp.float32,
     ).astype(jnp.bfloat16)
     qkv = qkv_rows.reshape(all_tokens, local_heads, 3, HEAD_DIM)
     key_rows = qkv[:, :, 1, :]

time: 242 us -> 264 us (1.091)
  blocking collectives: 30 us -> 102 us
  waiting for transfers between devices: 146 us -> 86.7 us
  starting transfers between devices: 5.34 us -> 12.5 us
  local copies, waits for them, and re-layouts: 9.27 us -> 12.1 us
    all_gather x1, blocking collectives: 16.2 us -> 87.8 us  [gathered_by_axis(): value = lax.all_gather(value, axis, axis=dim, tiled=True)]
    all_gather x1 -> x0, waiting for transfers between devices: 59.5 us -> none  [per_device(): lax.all_gather(normed, SEQ, axis=0, tiled=True)]
    all_to_all x0 -> x1, starting transfers between devices: none -> 7.21 us  [per_device(): lax.all_to_all(jnp.stack([normed] * lax.axis_size(SEQ)), SEQ, 0, 0)]
    another operation x0 -> x1, local copies, waits for them, and re-layouts: none -> 2.84 us  [per_device(): jnp.stack([normed] * lax.axis_size(SEQ))]
  transfers between devices with their start and end apart: 4 -> 4, of which waited for: 3 -> 2; matrix products, arithmetic and copies ran while one was open for 13% -> 12% of each run, Pallas kernels for 0% -> 0%
where the time goes in v1:
time: 264 us
  blocking collectives  102 us (39%)
  waiting for transfers between devices  86.7 us (33%)
  matrix products  25.9 us (10%)
  between operations  13.5 us (5%)
  starting transfers between devices  12.5 us (5%)
  local copies, waits for them, and re-layouts  12.1 us (5%)
  other arithmetic  9.05 us (3%)
    all_gather x1, blocking collectives, gathered_by_axis(): value = lax.all_gather(value, axis, axis=dim, tiled=True)  87.8 us
    all_gather x1, waiting for transfers between devices, per_device(): lax.all_gather(merged, SEQ, axis=0, tiled=True)  71.9 us
    all_gather x1, waiting for transfers between devices, gathered_by_axis(): value = lax.all_gather(value, axis, axis=dim, tiled=True)  14.7 us
    all_to_all x1, blocking collectives, per_device(): lax.all_to_all(column_block, SEQ, split_axis=0, concat_axis=1, tiled=True)  13.7 us
    dot_general x4, matrix products, masked_scores(): jnp.einsum('qhd,khd->hqk', queries, key_part, preferred_element_type=jnp....  7.64 us
    dot_general x4, matrix products, query_block(): jnp.einsum('hqk,khd->qhd', probs, value_rows, preferred_element_type=jnp....  7.48 us
    all_to_all x1, starting transfers between devices, per_device(): lax.all_to_all(jnp.stack([normed] * lax.axis_size(SEQ)), SEQ, 0, 0)  7.21 us
  transfers between devices with their start and end apart: 4, of which 2 were waited for; matrix products, arithmetic and copies ran while one was open for 12% of the time, Pallas kernels for 0%

profile of v1, /device:TPU:32, one launch (start us, length us, event | category | flops | bytes accessed | tf_op | source)
XLA Modules:
  0.0 263.7 jit_solution(2767742694268110489)
XLA Ops:
  6.5 1.2 convert_reduce_fusion
  10.2 2.8 %stack.2 = bf16[16,128,1280]{2,1,0:T(8,128)(2,1)} broadcast(bf16[128,1280]{1,0:T(8,128)(2,1)S(1)} %fusion.31), dimensions={1,2} | broadcast | bytes 5570560 | tf_op jit(solution)/shard_map/stack | solution.py:36
  13.1 7.2 %all-to-all-start = ((bf16[16,128,1280]{2,1,0:T(8,128)(2,1)}), bf16[16,128,1280]{2,1,0:T(8,128)(2,1)}, u32[]{:S(2)}, u32[]{:S(2)}) async-start(bf16[16,128,1280]{2,1,0:T(8,128)(2,1)} %stack.2), calls=%async_computation | async-start | bytes 10485760 | tf_op jit(solution)/shard_map/all_to_all | solution.py:36
  20.3 87.8 %all_gather.9 = bf16[320,1280]{1,0:T(8,128)(2,1)} all-gather(bf16[80,1280]{1,0:T(8,128)(2,1)S(1)} %copy-done.4), channel_id=1, replica_groups=mesh['dp'=32,'seq_0'=4,'seq_1'=4] {'seq_1'}, dimensions={0}, use_global_device_ids=true | all-gather | bytes 1024000 | tf_op jit(solution)/shard_map/all_gather | solution.py:16
  108.2 4.2 %convolution_convert_fusion = bf16[2048,240]{0,1:T(8,128)(2,1)S(1)} fusion(bf16[2048,1280]{1,0:T(8,128)(2,1)} %bitcast.8, bf16[1280,240]{0,1:T(8,128)(2,1)} %param.11), kind=kOutput, calls=%fused_computation.19 | convolution fusion | flops 1258782720 | bytes 6840320 | tf_op jit(solution)/shard_map/dot_general | solution.py:34
  113.5 25.1 %while.10 = (s32[]{:T(128)}, bf16[4,512,80]{1,2,0:T(8,128)(2,1)}, s32[4]{0:T(128)S(1)}, s32[2048]{0:T(1024)S(1)}, bf16[2048,1,3,80]{0,3,2,1:T(8,128)(2,1)}, /*in...) while((s32[]{:T(128)}, bf16[4,512,80]{1,2,0:T(8,128)(2,1)}, ...), condition=%wide.region_5.6_spmd, body=%wide.region_2.5_spmd.sunk | while | flops 352402432 | bytes 13447855 | solution.py:69
  114.8 1.9 fusion.46
  116.7 1.2 fusion.47
  117.9 1.9 fusion.48
  121.0 1.9 fusion.46
  124.2 1.9 fusion.48
  127.3 1.9 fusion.46
  129.2 1.2 fusion.47
  130.5 1.9 fusion.48
  133.6 1.9 fusion.46
  135.5 1.2 fusion.47
  136.7 1.9 fusion.48
  140.7 1.8 copy.16
  142.5 5.2 %all-to-all-start.1 = ((bf16[16,128,80]{1,2,0:T(8,128)(2,1)}), bf16[16,128,80]{1,2,0:T(8,128)(2,1)S(1)}, u32[]{:S(2)}, u32[]{:S(2)}) async-start(bf16[16,128,80]{1,2,0:T(8,128)(2,1)} %copy.16), calls=%async_computation.1 | async-start | bytes 655360 | tf_op jit(solution)/shard_map/all_to_all | solution.py:72
  147.8 14.7 %all-gather.3.cloned.1.call-done = bf16[1280,1280]{1,0:T(8,128)(2,1)} async-done(((bf16[320,1280]{1,0:T(8,128)(2,1)}), bf16[1280,1280]{1,0:T(8,128)(2,1)}) %all-gather.3.cloned.1.call-update) | async-done | bytes 3276816 | tf_op jit(solution)/shard_map/all_gather | solution.py:16
  162.5 2.6 %fusion.32 = (f32[128]{0:T(128)S(1)}, f32[128,1280]{1,0:T(8,128)S(1)}) fusion(bf16[128,1280]{0,1:T(8,128)(2,1)S(1)} %bitcast.65, bf16[1280,1280]{1,0:T(8,128)(2,1)} %all-gather.3.cloned.1.call-done, bf16[128,1280]{1,0:T(8,128)(2,1)S(1)} %copy-done.1), kind=kOutput, calls=%fused_computation.37 | convolution fusion | flops 419921792 | bytes 4588032 | tf_op jit(solution)/shard_map/dot_general | solution.py:73
  166.5 71.9 %all-gather.5.cloned.1.call-done = bf16[512,5120]{1,0:T(8,128)(2,1)} async-done(((bf16[32,5120]{1,0:T(8,128)(2,1)}), bf16[512,5120]{1,0:T(8,128)(2,1)}) %all-gather.5.cloned.1.call-update) | async-done | bytes 5242896 | tf_op jit(solution)/shard_map/all_gather | solution.py:80
  238.4 4.0 %convolution_convert_fusion.1 = bf16[512,256]{1,0:T(8,128)(2,1)S(1)} fusion(bf16[512,5120]{1,0:T(8,128)(2,1)} %all-gather.5.cloned.1.call-done, bf16[5120,256]{1,0:T(8,128)(2,1)S(1)} %copy-done), kind=kOutput, calls=%fused_computation.21 | convolution fusion | flops 1342308352 | bytes 8126464 | tf_op jit(solution)/shard_map/dot_general | solution.py:79
  242.4 13.7 %all_to_all.43 = bf16[16,32,256]{2,1,0:T(8,128)(2,1)S(1)} all-to-all(bf16[16,32,256]{2,1,0:T(8,128)(2,1)S(1)} %bitcast.69), channel_id=1, replica_groups=mesh['dp'=32,'seq_0'=4,'seq_1'=4] {'seq_0','seq_1'}, dimensions={0} | all-to-all | bytes 524288 | tf_op jit(solution)/shard_map/all_to_all | solution.py:82
  (42 shorter events, 11.7 us)
Async XLA Ops:
  6.5 231.9 %copy-start = (bf16[5120,256]{1,0:T(8,128)(2,1)S(1)}, bf16[5120,256]{1,0:T(8,128)(2,1)}, u32[]{:S(2)}) copy-start(bf16[5120,256]{1,0:T(8,128)(2,1)} %param.13) | copy-start | bytes 7864324
  13.1 7.3 %copy-start.4 = (bf16[80,1280]{1,0:T(8,128)(2,1)S(1)}, bf16[80,1280]{1,0:T(8,128)(2,1)}, u32[]{:S(2)}) copy-start(bf16[80,1280]{1,0:T(8,128)(2,1)} %param.12) | copy-start | bytes 614404
  13.1 95.2 %all-to-all-start = ((bf16[16,128,1280]{2,1,0:T(8,128)(2,1)}), bf16[16,128,1280]{2,1,0:T(8,128)(2,1)}, u32[]{:S(2)}, u32[]{:S(2)}) async-start(bf16[16,128,1280]{2,1,0:T(8,128)(2,1)} %stack.2), calls=%async_computation | async-start | bytes 10485760 | tf_op jit(solution)/shard_map/all_to_all | solution.py:36
  20.3 142.2 %all-gather.3.cloned.1.call-start = ((), (), s32[]{:S(2)}) async-start(), calls=%async_computation.3 | async-start | bytes 4096000 | tf_op jit(solution)/shard_map/all_gather | solution.py:16
  108.2 5.3 %copy-start.3 = (s32[2048]{0:T(1024)S(1)}, s32[2048]{0:T(1024)}, u32[]{:S(2)}) copy-start(s32[2048]{0:T(1024)} %param.10) | copy-start | bytes 24580
  112.4 1.1 copy-start.2
  113.5 49.0 %copy-start.1 = (bf16[128,1280]{1,0:T(8,128)(2,1)S(1)}, bf16[128,1280]{1,0:T(8,128)(2,1)}, u32[]{:S(2)}) copy-start(bf16[128,1280]{1,0:T(8,128)(2,1)} %param.9) | copy-start | bytes 983044
  138.6 26.7 %copy-start.5 = (f32[1280]{0:T(1024)S(1)}, f32[1280]{0:T(1024)}, u32[]{:S(2)}) copy-start(f32[1280]{0:T(1024)} %param.15) | copy-start | bytes 15364
  142.5 20.0 %all-to-all-start.1 = ((bf16[16,128,80]{1,2,0:T(8,128)(2,1)}), bf16[16,128,80]{1,2,0:T(8,128)(2,1)S(1)}, u32[]{:S(2)}, u32[]{:S(2)}) async-start(bf16[16,128,80]{1,2,0:T(8,128)(2,1)} %copy.16), calls=%async_computation.1 | async-start | bytes 655360 | tf_op jit(solution)/shard_map/all_to_all | solution.py:72
  147.7 90.7 %all-gather.5.cloned.1.call-start = ((), (), s32[]{:S(2)}) async-start(), calls=%async_computation.4 | async-start | bytes 5570560 | tf_op jit(solution)/shard_map/all_gather | solution.py:80
Sparse Core Ops, SparseCore 0:
  108.3 54.0 all-gather.2
  166.6 71.7 all-gather.4
